TPU v7x, 32 devices: a whole 2x2x4 slice. The times are simulated.
32 devices in a mesh: req: 4 (over z), mlp: 8 (over y, x, core).
Axes of the slice: x: 2, y: 2, z: 4, core: 2. Of those that a mesh axis runs over, the one named last changes fastest.
Arguments:
- tokens: bfloat16 [2048, 5120], P(('req', 'mlp')), may hold values from -6 to 6
- norm_scale: float32 [5120], replicated, may hold values from 0.25 to 1.75
- gate_matrix: bfloat16 [5120, 14336], P(None, 'mlp'), may hold values from -0.078125 to 0.078125
- up_matrix: bfloat16 [5120, 14336], P(None, 'mlp'), may hold values from -0.078125 to 0.078125
- down_matrix: bfloat16 [14336, 5120], P('mlp', 'req'), may hold values from -0.046875 to 0.046875
- adapter_down_maps: bfloat16 [8, 32, 5120], P('mlp'), may hold values from -0.078125 to 0.078125
- adapter_gate_up_out: bfloat16 [2, 128, 14336], P(None, None, 'mlp'), may hold values from -1.5 to 1.5
- adapter_down_proj_in: bfloat16 [128, 14336], P(None, 'mlp'), may hold values from -0.046875 to 0.046875
- adapter_down_proj_out: bfloat16 [128, 5120], replicated, may hold values from -1.5 to 1.5
- token_adapters: int32 [2048, 1], P(('req', 'mlp')), may hold values from 0 to 7; in each aligned block of 64 rows (0 to 63, 64 to 127, ...) at most 16 rows name the same one
Outputs:
- mixed: bfloat16 [2048, 5120], P(('req', 'mlp'))
Inputs may be any that keep to these rules, and one draw needn't show every extreme that they name: `token_adapters`: among the 64 rows of one device no adapter is named by more than 16 rows, and in every draw some device has an adapter named by exactly 16 of its rows.
All inputs are finite; a program needn't handle non-finite values.
Results may differ from a plain program's by a relative error of at most 0.013.
Values may be sent and summed in bfloat16 or wider, within the bound.
A program may use at most 192 MiB of HBM per device.

v0:
```python
import jax
import jax.numpy as jnp
from jax import lax
from jax.sharding import PartitionSpec as P

CAP = 16


EPS = 1e-06


def normalize(tokens, norm_scale):
    widened = tokens.astype(jnp.float32)
    mean_square = jnp.mean(widened * widened, axis=-1, keepdims=True)
    return (widened * lax.rsqrt(mean_square + EPS) * norm_scale).astype(jnp.bfloat16)


def rank_routed(normed_input, adapter_lookup, adapter_down_maps, owner_list):
    capacity = CAP
    chosen = (adapter_lookup[:, None] == jnp.arange(owner_list, dtype=jnp.int32)[None, :]).astype(
        jnp.int32
    )
    earlier = jnp.cumsum(chosen, axis=0) - chosen
    slot_of = jnp.sum(earlier * chosen, axis=1)
    target = adapter_lookup * capacity + slot_of
    dispatch = (
        jnp.arange(owner_list * capacity, dtype=jnp.int32)[:, None] == target[None, :]
    ).astype(jnp.bfloat16)
    outgoing = jnp.dot(dispatch, normed_input, preferred_element_type=jnp.float32).astype(
        jnp.bfloat16
    )
    outgoing = outgoing.reshape(owner_list, capacity, normed_input.shape[1])
    owner_table = adapter_down_maps[0]
    produced = jnp.einsum(
        "nkd,rd->nkr",
        lax.all_to_all(outgoing, "mlp", split_axis=0, concat_axis=0, tiled=True),
        owner_table,
        preferred_element_type=jnp.float32,
    ).astype(jnp.bfloat16)
    returned = lax.all_to_all(produced, "mlp", split_axis=0, concat_axis=0, tiled=True)
    returned = returned.reshape(owner_list * capacity, returned.shape[2])
    return lax.dot_general(
        dispatch, returned, (((0,), (0,)), ((), ())), preferred_element_type=jnp.float32
    ).astype(jnp.bfloat16)


def per_device(
    tokens,
    norm_scale,
    gate_matrix,
    up_matrix,
    down_matrix,
    adapter_down_maps,
    adapter_gate_up_out,
    adapter_down_proj_in,
    adapter_down_proj_out,
    token_adapters,
):
    owner_list = lax.axis_size("mlp")
    rank_span = adapter_down_maps.shape[1]
    half_rank = rank_span // 2
    normed_input = normalize(tokens, norm_scale)
    adapter_lookup = token_adapters[:, 0]
    gathered = lax.all_gather(normed_input, "mlp", axis=0, tiled=True)
    group_of = lax.all_gather(adapter_lookup, "mlp", axis=0, tiled=True)
    group_rows = gathered.shape[0]
    selector = group_of[:, None] == jnp.arange(owner_list, dtype=jnp.int32)[None, :]
    zero_half = jnp.zeros((), jnp.bfloat16)
    rank_per_token = rank_routed(normed_input, adapter_lookup, adapter_down_maps, owner_list)
    rank_rows = lax.all_gather(rank_per_token, "mlp", axis=0, tiled=True)
    spread = jnp.where(selector[:, :, None], rank_rows[:, None, :], zero_half)
    gate_rank_values = spread[:, :, :half_rank].reshape(group_rows, owner_list * half_rank)
    up_rank_values = spread[:, :, half_rank:].reshape(group_rows, owner_list * half_rank)
    gate_total = jnp.dot(gathered, gate_matrix, preferred_element_type=jnp.float32) + jnp.dot(
        gate_rank_values, adapter_gate_up_out[0], preferred_element_type=jnp.float32
    )
    up_total = jnp.dot(gathered, up_matrix, preferred_element_type=jnp.float32) + jnp.dot(
        up_rank_values, adapter_gate_up_out[1], preferred_element_type=jnp.float32
    )
    hidden_state = (jax.nn.silu(gate_total) * up_total).astype(jnp.bfloat16)
    rank_term = lax.dot_general(
        hidden_state,
        adapter_down_proj_in,
        (((1,), (1,)), ((), ())),
        preferred_element_type=jnp.float32,
    )
    picker = jnp.repeat(selector, half_rank, axis=1)
    rank_term = jnp.where(picker, rank_term, jnp.float32(0.0))
    down_term = jnp.dot(
        hidden_state,
        lax.all_gather(down_matrix, "req", axis=1, tiled=True),
        preferred_element_type=jnp.float32,
    )
    projected_down = lax.psum_scatter(
        down_term.astype(jnp.bfloat16), "mlp", scatter_dimension=0, tiled=True
    ).astype(jnp.float32)
    total_rank = lax.psum_scatter(
        rank_term.astype(jnp.bfloat16), "mlp", scatter_dimension=0, tiled=True
    )
    adapter_down_term = jnp.dot(
        total_rank, adapter_down_proj_out, preferred_element_type=jnp.float32
    )
    return (tokens.astype(jnp.float32) + projected_down + adapter_down_term).astype(jnp.bfloat16)


def solution(mesh):
    return jax.shard_map(
        per_device,
        mesh=mesh,
        in_specs=(
            P(("req", "mlp"), None),
            P(),
            P(None, "mlp"),
            P(None, "mlp"),
            P("mlp", "req"),
            P("mlp", None, None),
            P(None, None, "mlp"),
            P(None, "mlp"),
            P(),
            P(("req", "mlp"), None),
        ),
        out_specs=P(("req", "mlp"), None),
        check_vma=False,
    )
```

profile of v0, /device:TPU:19, one launch (start us, length us, event | category | flops | bytes accessed | tf_op | source)
XLA Modules:
  0.0 486.1 jit_solution(2720626967359429223)
XLA Ops:
  6.5 1.4 fusion.1
  8.0 2.2 fusion.3
  10.2 0.7 all-gather.7.cloned.1.call-update
  11.1 0.6 dynamic-slice
  12.7 1.5 convolution_convert_fusion.1
  14.2 4.6 all-to-all-start
  18.8 24.8 %all-reduce = s32[512]{0:T(512)S(1)} all-reduce(s32[512]{0:T(512)S(1)} %get-tuple-element.8), channel_id=2, replica_groups=mesh['req'=4,'mlp'=8] {'mlp'}, use_global_device_ids=true, to_apply=%add | all-reduce | flops 512 | bytes 4096
  43.6 2.1 convolution_convert_fusion.2
  45.7 1.4 reshape.71
  47.1 5.8 %all-to-all-start.1 = ((bf16[8,2,256]{2,1,0:T(2,128)(2,1)}), bf16[8,2,256]{2,1,0:T(2,128)(2,1)S(1)}, u32[]{:S(2)}, u32[]{:S(2)}) async-start(bf16[8,2,256]{2,1,0:T(2,128)(2,1)} %reshape.71), calls=%async_computation.1 | async-start | bytes 16384 | tf_op jit(solution)/shard_map/all_to_all | solution.py:40
  53.1 3.0 all-to-all-done.1
  56.2 0.2 fusion.5
  56.4 9.7 %all-gather.1 = bf16[8,64,32]{1,2,0:T(8,128)(2,1)S(1)} all-gather(bf16[1,64,32]{1,2,0:T(8,128)(2,1)S(1)} %fusion.5), channel_id=1, replica_groups=mesh['req'=4,'mlp'=8] {'mlp'}, dimensions={0}, use_global_device_ids=true | all-gather | bytes 36864 | tf_op jit(solution)/shard_map/all_gather | solution.py:70
  66.3 2.6 fusion.6
  68.9 2.4 fusion.8
  71.3 17.4 %fusion.17 = f32[512,1792]{1,0:T(8,128)} fusion(bf16[512,5120]{1,0:T(8,128)(2,1)} %all-gather.5.cloned.1.call-done, bf16[5120,1792]{1,0:T(8,128)(2,1)} %param.12), kind=kOutput, calls=%fused_computation.35 | convolution fusion | flops 9395240960 | bytes 27262976 | tf_op jit(solution)/shard_map/dot_general | solution.py:74
  88.7 17.4 %multiply_convert_fusion = bf16[512,1792]{1,0:T(8,128)(2,1)S(1)} fusion(f32[512,1792]{1,0:T(8,128)S(1)} %copy-done.3, f32[512,1792]{1,0:T(8,128)} %fusion.17, f32[512,1792]{1,0:T(8,128)S(1)} %copy-done.4, bf16[512,5120]{1,0:T(8,128)(2,1)} %all-gather.5.cloned.1.call-done, bf16[5120,1792]{1,0:T(8,128)(2,1)} %param.13), kind=kOutput, calls=%fused_computation.4 | convolution fusion | flops 9402580992 | bytes 36438016 | tf_op jit(solution)/shard_map/dot_general | solution.py:77
  106.1 1.3 fusion.4
  107.4 0.3 reduce-scatter.5.cloned.1.call-start
  107.7 273.0 %all-gather.7.cloned.1.call-done = bf16[1792,5120]{1,0:T(8,128)(2,1)} async-done(((bf16[1792,1280]{1,0:T(8,128)(2,1)}), bf16[1792,5120]{1,0:T(8,128)(2,1)}) %all-gather.7.cloned.1.call-update) | async-done | bytes 18350096 | tf_op jit(solution)/shard_map/all_gather | solution.py:91
  380.6 15.0 %convolution_convert_fusion = bf16[512,5120]{1,0:T(8,128)(2,1)} fusion(bf16[512,1792]{1,0:T(8,128)(2,1)S(1)} %multiply_convert_fusion, bf16[1792,5120]{1,0:T(8,128)(2,1)} %all-gather.7.cloned.1.call-done), kind=kOutput, calls=%fused_computation | convolution fusion | flops 9397862400 | bytes 25427968 | tf_op jit(solution)/shard_map/dot_general | solution.py:89
  395.6 20.9 %reduce-scatter.7.cloned.1.call-done = bf16[64,128]{1,0:T(8,128)(2,1)} async-done(((bf16[512,128]{1,0:T(8,128)(2,1)}), bf16[64,128]{1,0:T(8,128)(2,1)}) %reduce-scatter.7.cloned.1.call-update) | async-done | bytes 16400
  416.6 60.7 %reduce-scatter.5.cloned.1.call-done = bf16[64,5120]{1,0:T(8,128)(2,1)} async-done(((bf16[512,5120]{1,0:T(8,128)(2,1)}), bf16[64,5120]{1,0:T(8,128)(2,1)}) %reduce-scatter.5.cloned.1.call-update) | async-done | bytes 655376 | tf_op jit(solution)/shard_map/reduce_scatter | solution.py:94
  477.3 2.3 fusion
  (40 shorter events, 1.0 us)
Async XLA Ops:
  6.5 470.7 %copy-start = (bf16[128,5120]{1,0:T(8,128)(2,1)S(1)}, bf16[128,5120]{1,0:T(8,128)(2,1)}, u32[]{:S(2)}) copy-start(bf16[128,5120]{1,0:T(8,128)(2,1)} %param.18) | copy-start | bytes 3932164
  6.5 4.6 copy-start.8
  6.5 4.4 copy-start.7
  6.5 64.8 %all-gather.5.cloned.1.call-start = ((), (), s32[]{:S(2)}) async-start(), calls=%async_computation.4 | async-start | bytes 5898240 | tf_op jit(solution)/shard_map/all_gather | solution.py:64
  10.2 2.5 copy-start.1
  10.2 370.4 %all-gather.7.cloned.1.call-start = ((), (), s32[]{:S(2)}) async-start(), calls=%async_computation.5 | async-start | bytes 22937600 | tf_op jit(solution)/shard_map/all_gather | solution.py:91
  12.7 53.6 %copy-start.5 = (bf16[2,128,1792]{2,1,0:T(8,128)(2,1)S(1)}, bf16[2,128,1792]{2,1,0:T(8,128)(2,1)}, u32[]{:S(2)}) copy-start(bf16[2,128,1792]{2,1,0:T(8,128)(2,1)} %param.16) | copy-start | bytes 2752516
  14.2 29.4 %all-to-all-start = ((bf16[8,16,5120]{2,1,0:T(8,128)(2,1)}), bf16[8,16,5120]{2,1,0:T(8,128)(2,1)S(1)}, u32[]{:S(2)}, u32[]{:S(2)}) async-start(bf16[8,16,5120]{2,1,0:T(8,128)(2,1)} %bitcast.2), calls=%async_computation | async-start | bytes 2621440 | tf_op jit(solution)/shard_map/all_to_all | solution.py:36
  47.1 9.0 %all-to-all-start.1 = ((bf16[8,2,256]{2,1,0:T(2,128)(2,1)}), bf16[8,2,256]{2,1,0:T(2,128)(2,1)S(1)}, u32[]{:S(2)}, u32[]{:S(2)}) async-start(bf16[8,2,256]{2,1,0:T(2,128)(2,1)} %reshape.71), calls=%async_computation.1 | async-start | bytes 16384 | tf_op jit(solution)/shard_map/all_to_all | solution.py:40
  52.9 363.7 %reduce-scatter.7.cloned.1.call-start = ((), (), s32[]{:S(2)}) async-start(), calls=%async_computation.7 | async-start | bytes 147456
  71.3 17.4 %copy-start.3 = (f32[512,1792]{1,0:T(8,128)S(1)}, f32[512,1792]{1,0:T(8,128)}, u32[]{:S(2)}) copy-start(f32[512,1792]{1,0:T(8,128)} %fusion.6) | copy-start | bytes 11010052
  71.3 17.4 %copy-start.4 = (f32[512,1792]{1,0:T(8,128)S(1)}, f32[512,1792]{1,0:T(8,128)}, u32[]{:S(2)}) copy-start(f32[512,1792]{1,0:T(8,128)} %fusion.8) | copy-start | bytes 11010052
  88.7 17.4 %copy-start.6 = (bf16[128,1792]{1,0:T(8,128)(2,1)S(1)}, bf16[128,1792]{1,0:T(8,128)(2,1)}, u32[]{:S(2)}) copy-start(bf16[128,1792]{1,0:T(8,128)(2,1)} %param.17) | copy-start | bytes 1376260
  107.4 369.8 %reduce-scatter.5.cloned.1.call-start = ((), (), s32[]{:S(2)}) async-start(), calls=%async_computation.6 | async-start | bytes 5898240 | tf_op jit(solution)/shard_map/reduce_scatter | solution.py:94
  395.6 81.6 %copy-start.2 = (bf16[64,5120]{1,0:T(8,128)(2,1)S(1)}, bf16[64,5120]{1,0:T(8,128)(2,1)}, u32[]{:S(2)}) copy-start(bf16[64,5120]{1,0:T(8,128)(2,1)} %param.10) | copy-start | bytes 1966084
Sparse Core Ops, SparseCore 0:
  10.3 56.1 all-gather.4
  68.1 312.5 all-gather.6
  383.6 32.8 reduce-scatter.6
  420.2 57.0 reduce-scatter.4
where the time goes:
time: 488 us; the launch traced here: 486 us
  waiting for transfers between devices  358 us (73%)
  matrix products  62.1 us (13%)
  blocking collectives  34.5 us (7%)
  between operations  13.9 us (3%)
  starting transfers between devices  10.7 us (2%)
    all_gather x1, waiting for transfers between devices, per_device(): lax.all_gather(down_matrix, 'req', axis=1, tiled=True)  273 us
    reduce_scatter x1, waiting for transfers between devices, per_device(): lax.psum_scatter(down_term.astype(jnp.bfloat16), 'mlp', scatter_dimension...  60.7 us
    unnamed x1, blocking collectives  24.8 us
    unnamed x5, waiting for transfers between devices  21.7 us
    dot_general x1, matrix products, per_device(): jnp.dot(gathered, up_matrix, preferred_element_type=jnp.float32)  17.4 us
    dot_general x1, matrix products, per_device(): jnp.dot(gathered, gate_matrix, preferred_element_type=jnp.float32)  17.4 us
    dot_general x1, matrix products, per_device(): jnp.dot(hidden_state, lax.all_gather(down_matrix, 'req', axis=1, tiled=Tr...  15 us
  transfers between devices with their start and end apart: 6, of which 4 were waited for; matrix products, arithmetic and copies ran while one was open for 13% of the time, Pallas kernels for 0%

commit v1 on v0

--- a/solution.py
+++ b/solution.py
@@ -86,13 +86,18 @@
     )
     picker = jnp.repeat(selector, half_rank, axis=1)
     rank_term = jnp.where(picker, rank_term, jnp.float32(0.0))
+    req_count = lax.axis_size("req")
+    token_rows = tokens.shape[0]
+    columns = down_matrix.shape[1]
+    hidden_everywhere = lax.all_gather(hidden_state, "req", axis=0, tiled=True)
     down_term = jnp.dot(
-        hidden_state,
-        lax.all_gather(down_matrix, "req", axis=1, tiled=True),
-        preferred_element_type=jnp.float32,
-    )
-    projected_down = lax.psum_scatter(
-        down_term.astype(jnp.bfloat16), "mlp", scatter_dimension=0, tiled=True
+        hidden_everywhere, down_matrix, preferred_element_type=jnp.float32
+    ).astype(jnp.bfloat16)
+    down_term = down_term.reshape(req_count, owner_list, token_rows, columns)
+    down_term = down_term.transpose(1, 0, 2, 3).reshape(-1, columns)
+    projected_down = lax.psum_scatter(down_term, "mlp", scatter_dimension=0, tiled=True)
+    projected_down = lax.all_to_all(
+        projected_down, "req", split_axis=0, concat_axis=1, tiled=True
     ).astype(jnp.float32)
     total_rank = lax.psum_scatter(
         rank_term.astype(jnp.bfloat16), "mlp", scatter_dimension=0, tiled=True

time: 488 us -> 363 us (0.74)
  waiting for transfers between devices: 358 us -> 224 us
    all_gather x1, waiting for transfers between devices: 273 us -> 130 us  [per_device(): hidden_everywhere = lax.all_gather(hidden_state, 'req', axis=0, tiled=True)]
    all_to_all x0 -> x1, waiting for transfers between devices: none -> 11.3 us  [per_device(): lax.all_to_all(projected_down, 'req', split_axis=0, concat_axis=1, tiled=...]
  transfers between devices with their start and end apart: 6 -> 7, of which waited for: 4 -> 5; matrix products, arithmetic and copies ran while one was open for 13% -> 5% of each run, Pallas kernels for 0% -> 0%
where the time goes in v1:
time: 363 us; the launch traced here: 360 us
  waiting for transfers between devices  224 us (62%)
  matrix products  62.2 us (17%)
  blocking collectives  32 us (9%)
  starting transfers between devices  15.1 us (4%)
  between operations  13.8 us (4%)
  other arithmetic  7.21 us (2%)
  local copies, waits for them, and re-layouts  5.88 us (2%)
    all_gather x1, waiting for transfers between devices, per_device(): hidden_everywhere = lax.all_gather(hidden_state, 'req', axis=0, tiled=True)  130 us
    reduce_scatter x1, waiting for transfers between devices, per_device(): lax.psum_scatter(down_term, 'mlp', scatter_dimension=0, tiled=True)  56.7 us
    unnamed x1, blocking collectives  22.5 us
    unnamed x5, waiting for transfers between devices  22.3 us
    dot_general x1, matrix products, per_device(): jnp.dot(gathered, up_matrix, preferred_element_type=jnp.float32)  18.2 us
    dot_general x1, matrix products, per_device(): jnp.dot(gathered, gate_matrix, preferred_element_type=jnp.float32)  16.2 us
    dot_general x1, matrix products, per_device(): jnp.dot(hidden_everywhere, down_matrix, preferred_element_type=jnp.float32)  13.2 us
    all_to_all x1, waiting for transfers between devices, per_device(): lax.all_to_all(projected_down, 'req', split_axis=0, concat_axis=1, tiled=...  11.3 us
  transfers between devices with their start and end apart: 7, of which 5 were waited for; matrix products, arithmetic and copies ran while one was open for 5% of the time, Pallas kernels for 0%

profile of v1, /device:TPU:19, one launch (start us, length us, event | category | flops | bytes accessed | tf_op | source)
XLA Modules:
  0.0 359.9 jit_solution(1677360773098772335)
XLA Ops:
  6.5 1.4 fusion.1
  8.0 2.2 fusion.3
  11.0 1.2 dynamic-slice
  14.4 2.8 convolution_convert_fusion.1
  17.2 4.6 %all-to-all-start = ((bf16[8,16,5120]{2,1,0:T(8,128)(2,1)}), bf16[8,16,5120]{2,1,0:T(8,128)(2,1)S(1)}, u32[]{:S(2)}, u32[]{:S(2)}) async-start(bf16[8,16,5120]{2,1,0:T(8,128)(2,1)} %bitcast.2), calls=%async_computation | async-start | bytes 2621440 | tf_op jit(solution)/shard_map/all_to_all | solution.py:36
  21.7 22.5 %all-reduce = s32[512]{0:T(512)S(1)} all-reduce(s32[512]{0:T(512)S(1)} %get-tuple-element.8), channel_id=2, replica_groups=mesh['req'=4,'mlp'=8] {'mlp'}, use_global_device_ids=true, to_apply=%add | all-reduce | flops 512 | bytes 4096
  44.2 2.1 convolution_convert_fusion.2
  46.3 1.4 reshape.85
  47.7 5.7 %all-to-all-start.1 = ((bf16[8,2,256]{2,1,0:T(2,128)(2,1)}), bf16[8,2,256]{2,1,0:T(2,128)(2,1)S(1)}, u32[]{:S(2)}, u32[]{:S(2)}) async-start(bf16[8,2,256]{2,1,0:T(2,128)(2,1)} %reshape.85), calls=%async_computation.1 | async-start | bytes 16384 | tf_op jit(solution)/shard_map/all_to_all | solution.py:40
  53.4 3.3 all-to-all-done.1
  57.0 9.6 %all-gather.1 = bf16[8,64,32]{1,2,0:T(8,128)(2,1)S(1)} all-gather(bf16[1,64,32]{1,2,0:T(8,128)(2,1)S(1)} %fusion.5), channel_id=1, replica_groups=mesh['req'=4,'mlp'=8] {'mlp'}, dimensions={0}, use_global_device_ids=true | all-gather | bytes 36864 | tf_op jit(solution)/shard_map/all_gather | solution.py:70
  66.8 2.5 fusion.6
  69.3 2.4 fusion.8
  71.7 16.2 %fusion.17 = f32[512,1792]{1,0:T(8,128)} fusion(bf16[512,5120]{1,0:T(8,128)(2,1)} %all-gather.5.cloned.1.call-done, bf16[5120,1792]{1,0:T(8,128)(2,1)} %param.12), kind=kOutput, calls=%fused_computation.36 | convolution fusion | flops 9395240960 | bytes 27262976 | tf_op jit(solution)/shard_map/dot_general | solution.py:74
  87.9 18.2 %multiply_convert_fusion = bf16[512,1792]{1,0:T(8,128)(2,1)} fusion(f32[512,1792]{1,0:T(8,128)S(1)} %copy-done.2, f32[512,1792]{1,0:T(8,128)} %fusion.17, f32[512,1792]{1,0:T(8,128)S(1)} %copy-done.3, bf16[512,5120]{1,0:T(8,128)(2,1)} %all-gather.5.cloned.1.call-done, bf16[5120,1792]{1,0:T(8,128)(2,1)} %param.13), kind=kOutput, calls=%fused_computation.4 | convolution fusion | flops 9402580992 | bytes 36438016 | tf_op jit(solution)/shard_map/dot_general | solution.py:77
  106.5 130.1 %all-gather.7.cloned.1.call-done = bf16[2048,1792]{1,0:T(8,128)(2,1)} async-done(((bf16[512,1792]{1,0:T(8,128)(2,1)}), bf16[2048,1792]{1,0:T(8,128)(2,1)}) %all-gather.7.cloned.1.call-update) | async-done | bytes 7340048 | tf_op jit(solution)/shard_map/all_gather | solution.py:92
  236.6 13.2 %convolution_convert_fusion = bf16[2048,1280]{1,0:T(8,128)(2,1)S(1)} fusion(bf16[2048,1792]{1,0:T(8,128)(2,1)} %all-gather.7.cloned.1.call-done, bf16[1792,1280]{1,0:T(8,128)(2,1)} %param.14), kind=kOutput, calls=%fused_computation | convolution fusion | flops 9397862400 | bytes 17170432 | tf_op jit(solution)/shard_map/dot_general | solution.py:93
  249.8 2.6 copy.15
  252.5 56.7 %reduce-scatter.5.cloned.1.call-done = bf16[256,1280]{1,0:T(8,128)(2,1)} async-done(((bf16[2048,1280]{1,0:T(8,128)(2,1)}), bf16[256,1280]{1,0:T(8,128)(2,1)}) %reduce-scatter.5.cloned.1.call-update) | async-done | bytes 655376 | tf_op jit(solution)/shard_map/reduce_scatter | solution.py:98
  309.2 4.6 %all-to-all-start.2 = ((bf16[4,64,1280]{2,1,0:T(8,128)(2,1)}), bf16[4,64,1280]{2,1,0:T(8,128)(2,1)}, u32[]{:S(2)}, u32[]{:S(2)}) async-start(bf16[4,64,1280]{2,1,0:T(8,128)(2,1)} %bitcast.51), calls=%async_computation.3 | async-start | bytes 1310720 | tf_op jit(solution)/shard_map/all_to_all | solution.py:99
  313.9 2.3 fusion.4
  316.3 11.3 %all-to-all-done.2 = bf16[4,64,1280]{2,1,0:T(8,128)(2,1)} async-done(((bf16[4,64,1280]{2,1,0:T(8,128)(2,1)}), bf16[4,64,1280]{2,1,0:T(8,128)(2,1)}, u32[]{:S(2)}, u32[]{:S(2)}) %all-to-all-start.2) | async-done | bytes 655392 | tf_op jit(solution)/shard_map/all_to_all | solution.py:99
  328.9 22.2 %reduce-scatter.7.cloned.1.call-done = bf16[64,128]{1,0:T(8,128)(2,1)} async-done(((bf16[512,128]{1,0:T(8,128)(2,1)}), bf16[64,128]{1,0:T(8,128)(2,1)}) %reduce-scatter.7.cloned.1.call-update) | async-done | bytes 16400
  351.1 2.3 fusion
  (37 shorter events, 4.7 us)
Async XLA Ops:
  6.5 344.5 %copy-start = (bf16[128,5120]{1,0:T(8,128)(2,1)S(1)}, bf16[128,5120]{1,0:T(8,128)(2,1)}, u32[]{:S(2)}) copy-start(bf16[128,5120]{1,0:T(8,128)(2,1)} %param.18) | copy-start | bytes 3932164
  6.5 65.2 %all-gather.5.cloned.1.call-start = ((), (), s32[]{:S(2)}) async-start(), calls=%async_computation.5 | async-start | bytes 5898240 | tf_op jit(solution)/shard_map/all_gather | solution.py:64
  14.4 52.4 %copy-start.4 = (bf16[2,128,1792]{2,1,0:T(8,128)(2,1)S(1)}, bf16[2,128,1792]{2,1,0:T(8,128)(2,1)}, u32[]{:S(2)}) copy-start(bf16[2,128,1792]{2,1,0:T(8,128)(2,1)} %param.16) | copy-start | bytes 2752516
  17.2 27.0 %all-to-all-start = ((bf16[8,16,5120]{2,1,0:T(8,128)(2,1)}), bf16[8,16,5120]{2,1,0:T(8,128)(2,1)S(1)}, u32[]{:S(2)}, u32[]{:S(2)}) async-start(bf16[8,16,5120]{2,1,0:T(8,128)(2,1)} %bitcast.2), calls=%async_computation | async-start | bytes 2621440 | tf_op jit(solution)/shard_map/all_to_all | solution.py:36
  47.7 9.0 %all-to-all-start.1 = ((bf16[8,2,256]{2,1,0:T(2,128)(2,1)}), bf16[8,2,256]{2,1,0:T(2,128)(2,1)S(1)}, u32[]{:S(2)}, u32[]{:S(2)}) async-start(bf16[8,2,256]{2,1,0:T(2,128)(2,1)} %reshape.85), calls=%async_computation.1 | async-start | bytes 16384 | tf_op jit(solution)/shard_map/all_to_all | solution.py:40
  53.4 183.1 %all-gather.7.cloned.1.call-start = ((), (), s32[]{:S(2)}) async-start(), calls=%async_computation.6 | async-start | bytes 9175040 | tf_op jit(solution)/shard_map/all_gather | solution.py:92
  71.7 16.2 %copy-start.2 = (f32[512,1792]{1,0:T(8,128)S(1)}, f32[512,1792]{1,0:T(8,128)}, u32[]{:S(2)}) copy-start(f32[512,1792]{1,0:T(8,128)} %fusion.6) | copy-start | bytes 11010052
  71.7 16.2 %copy-start.3 = (f32[512,1792]{1,0:T(8,128)S(1)}, f32[512,1792]{1,0:T(8,128)}, u32[]{:S(2)}) copy-start(f32[512,1792]{1,0:T(8,128)} %fusion.8) | copy-start | bytes 11010052
  106.2 203.0 %reduce-scatter.5.cloned.1.call-start = ((), (), s32[]{:S(2)}) async-start(), calls=%async_computation.7 | async-start | bytes 5898240 | tf_op jit(solution)/shard_map/reduce_scatter | solution.py:98
  252.5 61.5 %copy-start.1 = (bf16[512,1792]{1,0:T(8,128)(2,1)S(1)}, bf16[512,1792]{1,0:T(8,128)(2,1)}, u32[]{:S(2)}) copy-start(bf16[512,1792]{1,0:T(8,128)(2,1)} %multiply_convert_fusion) | copy-start | bytes 5505028
  309.2 18.4 %all-to-all-start.2 = ((bf16[4,64,1280]{2,1,0:T(8,128)(2,1)}), bf16[4,64,1280]{2,1,0:T(8,128)(2,1)}, u32[]{:S(2)}, u32[]{:S(2)}) async-start(bf16[4,64,1280]{2,1,0:T(8,128)(2,1)} %bitcast.51), calls=%async_computation.3 | async-start | bytes 1310720 | tf_op jit(solution)/shard_map/all_to_all | solution.py:99
  313.8 37.3 %reduce-scatter.7.cloned.1.call-start = ((), (), s32[]{:S(2)}) async-start(), calls=%async_computation.8 | async-start | bytes 147456
Sparse Core Ops, SparseCore 0:
  10.3 54.7 all-gather.4
  106.3 130.2 all-gather.6
  252.6 56.5 reduce-scatter.4
  317.5 33.4 reduce-scatter.6

commit v2 on v0

v2 whole, which is shorter than its diff:
```python
import functools

import jax
import jax.numpy as jnp
from jax import lax
from jax.experimental import pallas as pl
from jax.experimental.pallas import tpu as pltpu
from jax.sharding import PartitionSpec as P

EPS = 1e-06
MESH = pl.DeviceIdType.MESH
F32 = jnp.float32
BF16 = jnp.bfloat16


def tile_of(width):
    return 256 if width % 256 == 0 else 128


def block_kernel(
    n_req,
    n_mlp,
    tokens,
    scale,
    names,
    gate_hbm,
    up_hbm,
    down_hbm,
    maps,
    ups,
    downs_in,
    downs_out,
    out,
    parts,
    x_all,
    a_all,
    w_gate,
    w_up,
    w_down,
    hid,
    acc,
    piece,
    z_in,
    rk_out,
    rk_in,
    w_sem,
    d_sem,
    c_sem,
    a_send,
    a_recv,
    x_send,
    x_recv,
    h_send,
    h_recv,
    p_send,
    p_recv,
    k_send,
    k_recv,
    e_send,
    e_recv,
):
    r = lax.axis_index("req")
    m = lax.axis_index("mlp")
    rows, dim = tokens.shape
    hidden = gate_hbm.shape[1]
    columns = down_hbm.shape[1]
    span = maps.shape[0]
    half = span // 2
    bits = n_mlp.bit_length() - 1
    tile = tile_of(hidden)
    tiles = hidden // tile
    group = n_req * rows

    def flip(index, bit):
        power = 1 << bit
        return index + power * (1 - 2 * ((index // power) % 2))

    def peer(slot):
        index = m
        for stage in range(bits):
            if (slot >> stage) & 1:
                index = flip(index, (stage + 1) % bits)
        return index

    def weight_copies(t):
        at = pl.ds(pl.multiple_of(t * tile, tile), tile)
        return (
            pltpu.make_async_copy(gate_hbm.at[:, at], w_gate.at[:, at], w_sem.at[0, t]),
            pltpu.make_async_copy(up_hbm.at[:, at], w_up.at[:, at], w_sem.at[1, t]),
        )

    for t in range(tiles):
        for copy in weight_copies(t):
            copy.start()
    down_copy = pltpu.make_async_copy(down_hbm, w_down, d_sem)
    down_copy.start()

    barrier = pltpu.get_barrier_semaphore()
    for slot in range(1, n_mlp):
        pl.semaphore_signal(barrier, inc=1, device_id=(r, peer(slot)), device_id_type=MESH)
    for step in range(1, n_req):
        pl.semaphore_signal(
            barrier, inc=1, device_id=((r + step) % n_req, m), device_id_type=MESH
        )
    pl.semaphore_wait(barrier, n_mlp - 1 + n_req - 1)

    def remote(src, dst, send, recv, device):
        return pltpu.make_async_remote_copy(
            src_ref=src,
            dst_ref=dst,
            send_sem=send,
            recv_sem=recv,
            device_id=device,
            device_id_type=MESH,
        )

    own_maps = pl.ds(pl.multiple_of(m * span, span), span)
    map_copies = [
        remote(maps, a_all.at[own_maps, :], a_send.at[s], a_recv.at[s], (r, peer(s)))
        for s in range(1, n_mlp)
    ]
    for copy in map_copies:
        copy.start()
    a_all[own_maps, :] = maps[...]

    def norm_step(i, carry):
        at = pl.ds(pl.multiple_of(i * 16, 16), 16)
        wide = tokens[at, :].astype(F32)
        mean_square = jnp.mean(wide * wide, axis=-1, keepdims=True)
        x_all[at, 0:dim] = (wide * lax.rsqrt(mean_square + EPS) * scale[...]).astype(BF16)
        x_all[at, dim : dim + 128] = jnp.broadcast_to(
            names[at, :].astype(F32), (16, 128)
        ).astype(BF16)
        return carry

    lax.fori_loop(0, rows // 16, norm_step, 0)

    def gather_copy(stage):
        size = rows << stage
        return remote(
            x_all.at[pl.ds(0, size), :],
            x_all.at[pl.ds(size, size), :],
            x_send.at[stage],
            x_recv.at[stage],
            (r, flip(m, (stage + 1) % bits)),
        )

    gather_copy(0).start()
    for copy in map_copies:
        copy.wait_recv()

    def hop(way, step, slot):
        at = pl.ds(slot * rows, rows)
        sign = 1 if way == 0 else -1
        block = r - sign * (step - 1)
        ok = (block >= 0) & (block <= n_req - 1) & (r + sign >= 0) & (r + sign <= n_req - 1)

        def make():
            return remote(
                hid.at[block, at, :],
                hid.at[block, at, :],
                h_send.at[way, step - 1, slot],
                h_recv.at[way, step - 1, slot],
                (r + sign, m),
            )

        return ok, make

    def hop_start(way, step, slot):
        ok, make = hop(way, step, slot)

        @pl.when(ok)
        def _():
            make().start()

    def hop_arrival(way, step, slot):
        at = pl.ds(slot * rows, rows)
        sign = 1 if way == 0 else -1
        block = r - sign * step

        @pl.when((block >= 0) & (block <= n_req - 1))
        def _():
            remote(
                hid.at[block, at, :],
                hid.at[block, at, :],
                h_send.at[way, step - 1, slot],
                h_recv.at[way, step - 1, slot],
                (r - sign, m),
            ).wait_recv()

    def tick(k):
        for step in range(n_req - 1, 0, -1):
            slot = k - step
            if 0 <= slot < n_mlp:
                for way in (0, 1):
                    hop_arrival(way, step, slot)
                    if step < n_req - 1:
                        hop_start(way, step + 1, slot)

    def rank_copy(slot):
        return remote(
            rk_out.at[slot], rk_in.at[slot], k_send.at[slot], k_recv.at[slot], (r, peer(slot))
        )

    def compute(first, count, wait):
        size = count * rows
        at = pl.ds(first * rows, size)
        normed = x_all[at, 0:dim]
        adapter = x_all[at, dim : dim + 128].astype(F32)[:, 0:1]
        ranks = lax.dot_general(
            normed, a_all[...], (((1,), (1,)), ((), ())), preferred_element_type=F32
        )
        lane = lax.broadcasted_iota(jnp.int32, ranks.shape, 1)
        mine = adapter == (lane // span).astype(F32)
        low = (lane // half) % 2 == 0
        gate_ranks = jnp.where(mine & low, ranks, 0.0).astype(BF16)
        up_ranks = jnp.where(mine & jnp.logical_not(low), ranks, 0.0).astype(BF16)

        def step(t, carry):
            if wait:
                for copy in weight_copies(t):
                    copy.wait()
            cols = pl.ds(pl.multiple_of(t * tile, tile), tile)
            table = ups[:, cols]
            gate_sum = jnp.dot(
                x_all[at, 0:dim], w_gate[:, cols], preferred_element_type=F32
            ) + jnp.dot(gate_ranks, table, preferred_element_type=F32)
            up_sum = jnp.dot(
                x_all[at, 0:dim], w_up[:, cols], preferred_element_type=F32
            ) + jnp.dot(up_ranks, table, preferred_element_type=F32)
            value = gate_sum / (1.0 + jnp.exp(-gate_sum)) * up_sum
            hid[r, at, cols] = value.astype(BF16)
            return carry

        lax.fori_loop(0, tiles, step, 0)
        for slot in range(first, first + count):
            hop_start(0, 1, slot)
            hop_start(1, 1, slot)
        terms = lax.dot_general(
            hid[r, at, :], downs_in[...], (((1,), (1,)), ((), ())), preferred_element_type=F32
        )
        lane = lax.broadcasted_iota(jnp.int32, terms.shape, 1)
        terms = jnp.where(adapter == (lane // half).astype(F32), terms, 0.0).astype(BF16)
        for slot in range(first, first + count):
            low_row = (slot - first) * rows
            term = terms[low_row : low_row + rows]
            if slot == 0:
                rk_in[0] = term
            else:
                rk_out[slot] = term
                rank_copy(slot).start()

    compute(0, 1, True)
    done = 0
    for stage in range(bits):
        gather_copy(stage).wait_recv()
        if stage + 1 < bits:
            gather_copy(stage + 1).start()
        compute(1 << stage, 1 << stage, False)
        if stage + 1 < bits:
            done = done + 1
            tick(done)

    down_copy.wait()
    narrow = tile_of(columns)

    def staging(slot):
        low_row = slot * group
        if low_row + group <= dim:
            return w_gate.at[pl.ds(low_row, group), pl.ds(0, columns)]
        low_row = (slot - dim // group) * group
        return w_up.at[pl.ds(low_row, group), pl.ds(0, columns)]

    def part_copy(slot):
        return remote(
            staging(slot), parts.at[slot], p_send.at[slot], p_recv.at[slot], (r, peer(slot))
        )

    def down(slot):
        place = staging(slot)
        at = pl.ds(slot * rows, rows)

        def step(t, carry):
            cols = pl.ds(pl.multiple_of(t * narrow, narrow), narrow)
            left = hid[:, at, :].reshape(group, hidden)
            term = jnp.dot(left, w_down[:, cols], preferred_element_type=F32).astype(BF16)
            if slot == 0:
                acc[:, cols] = term.astype(F32)
            else:
                place[:, cols] = term
            return carry

        lax.fori_loop(0, columns // narrow, step, 0)
        if slot > 0:
            part_copy(slot).start()

    def collect(slot):
        part_copy(slot).wait_recv()
        copy = pltpu.make_async_copy(parts.at[slot], piece, c_sem)
        copy.start()
        copy.wait()
        acc[...] += piece[...].astype(F32)

    finished = 0
    for k in range(done, n_mlp + n_req - 1):
        if k > done:
            tick(k)
        while finished <= k - (n_req - 1) and finished < n_mlp:
            down(finished)
            if finished >= 3:
                collect(finished - 2)
            finished += 1
    for slot in range(max(1, n_mlp - 2), n_mlp):
        collect(slot)

    piece[...] = acc[...].astype(BF16)

    def exchange(step):
        target = (r + step) % n_req
        return remote(
            piece.at[pl.ds(pl.multiple_of(target * rows, rows), rows), :],
            z_in.at[r],
            e_send.at[step],
            e_recv.at[step],
            (target, m),
        )

    for step in range(1, n_req):
        exchange(step).start()
    z_in[r] = piece[pl.ds(pl.multiple_of(r * rows, rows), rows), :]
    total = rk_in[0].astype(F32)
    for slot in range(1, n_mlp):
        rank_copy(slot).wait_recv()
        total = total + rk_in[slot].astype(F32)
    total = total.astype(BF16)
    for step in range(1, n_req):
        source = (r + n_req - step) % n_req
        remote(
            piece.at[pl.ds(0, rows), :],
            z_in.at[source],
            e_send.at[step],
            e_recv.at[step],
            (source, m),
        ).wait_recv()
    for c in range(n_req):
        cols = slice(c * columns, (c + 1) * columns)
        out[:, cols] = (
            tokens[:, cols].astype(F32)
            + z_in[c].astype(F32)
            + jnp.dot(total, downs_out[:, cols], preferred_element_type=F32)
        ).astype(BF16)

    for copy in map_copies:
        copy.wait_send()
    for stage in range(bits):
        gather_copy(stage).wait_send()
    for slot in range(n_mlp):
        for way in (0, 1):
            for step in range(1, n_req):
                ok, make = hop(way, step, slot)

                @pl.when(ok)
                def _():
                    make().wait_send()

    for slot in range(1, n_mlp):
        rank_copy(slot).wait_send()
        part_copy(slot).wait_send()
    for step in range(1, n_req):
        exchange(step).wait_send()


def per_device(
    tokens,
    norm_scale,
    gate_matrix,
    up_matrix,
    down_matrix,
    adapter_down_maps,
    adapter_gate_up_out,
    adapter_down_proj_in,
    adapter_down_proj_out,
    token_adapters,
):
    n_req, n_mlp = lax.axis_size("req"), lax.axis_size("mlp")
    rows, dim = tokens.shape
    hidden = gate_matrix.shape[1]
    columns = down_matrix.shape[1]
    span = adapter_down_maps.shape[1]
    half = span // 2
    ranks = adapter_down_proj_in.shape[0]
    bits = n_mlp.bit_length() - 1
    group = n_req * rows
    ups = adapter_gate_up_out.reshape(2, n_mlp, half, hidden)
    ups = ups.transpose(1, 0, 2, 3).reshape(n_mlp * span, hidden)
    vmem = pl.BlockSpec(memory_space=pltpu.VMEM)
    hbm = pl.BlockSpec(memory_space=pltpu.HBM)
    dma = pltpu.SemaphoreType.DMA
    out, _ = pl.pallas_call(
        functools.partial(block_kernel, n_req, n_mlp),
        out_shape=(
            jax.ShapeDtypeStruct((rows, dim), BF16),
            jax.ShapeDtypeStruct((n_mlp, group, columns), BF16),
        ),
        in_specs=[vmem, vmem, vmem, hbm, hbm, hbm, vmem, vmem, vmem, vmem],
        out_specs=(vmem, hbm),
        scratch_shapes=[
            pltpu.VMEM((n_mlp * rows, dim + 128), BF16),
            pltpu.VMEM((n_mlp * span, dim), BF16),
            pltpu.VMEM((dim, hidden), BF16),
            pltpu.VMEM((dim, hidden), BF16),
            pltpu.VMEM((hidden, columns), BF16),
            pltpu.VMEM((n_req, n_mlp * rows, hidden), BF16),
            pltpu.VMEM((group, columns), F32),
            pltpu.VMEM((group, columns), BF16),
            pltpu.VMEM((n_req, rows, columns), BF16),
            pltpu.VMEM((n_mlp, rows, ranks), BF16),
            pltpu.VMEM((n_mlp, rows, ranks), BF16),
            dma((2, hidden // tile_of(hidden))),
            dma,
            dma,
            dma((n_mlp,)),
            dma((n_mlp,)),
            dma((bits,)),
            dma((bits,)),
            dma((2, n_req - 1, n_mlp)),
            dma((2, n_req - 1, n_mlp)),
            dma((n_mlp,)),
            dma((n_mlp,)),
            dma((n_mlp,)),
            dma((n_mlp,)),
            dma((n_req,)),
            dma((n_req,)),
        ],
        compiler_params=pltpu.CompilerParams(
            collective_id=0, has_side_effects=True, vmem_limit_bytes=67043328
        ),
    )(
        tokens,
        norm_scale.reshape(1, dim),
        token_adapters,
        gate_matrix,
        up_matrix,
        down_matrix,
        adapter_down_maps[0],
        ups,
        adapter_down_proj_in,
        adapter_down_proj_out,
    )
    return out


def solution(mesh):
    return jax.shard_map(
        per_device,
        mesh=mesh,
        in_specs=(
            P(("req", "mlp"), None),
            P(),
            P(None, "mlp"),
            P(None, "mlp"),
            P("mlp", "req"),
            P("mlp", None, None),
            P(None, None, "mlp"),
            P(None, "mlp"),
            P(),
            P(("req", "mlp"), None),
        ),
        out_specs=P(("req", "mlp"), None),
        check_vma=False,
    )
```

time: 488 us -> 237 us (0.49)
  waiting for transfers between devices: 358 us -> 0 us
  Pallas kernels: 0 us -> 231 us
  matrix products: 62.1 us -> 0 us
  blocking collectives: 34.5 us -> 0 us
  between operations: 13.9 us -> 0.01 us
  starting transfers between devices: 10.7 us -> 0 us
    all_gather x2 -> x0, waiting for transfers between devices: 273 us -> none  [the longest x1 273 us: per_device(): lax.all_gather(down_matrix, 'req', axis=1, tiled=True)]
    pallas_call x0 -> x1, Pallas kernels: none -> 231 us  [per_device(): pl.pallas_call(functools.partial(block_kernel, n_req, n_mlp), out_shape=(...]
    dot_general x10 -> x0, matrix products: 62.1 us -> none  [the longest x1 17.4 us: per_device(): jnp.dot(gathered, up_matrix, preferred_element_type=jnp.float32)]
    reduce_scatter x1 -> x0, waiting for transfers between devices: 60.7 us -> none  [per_device(): lax.psum_scatter(down_term.astype(jnp.bfloat16), 'mlp', scatter_dimension...]
    unnamed x1 -> x0, blocking collectives: 24.8 us -> none
    unnamed x5 -> x0, waiting for transfers between devices: 21.7 us -> none
    all_to_all x2 -> x0, starting transfers between devices: 10.4 us -> none  [the longest x1 5.79 us: rank_routed(): lax.all_to_all(produced, 'mlp', split_axis=0, concat_axis=0, tiled=True)]
    all_gather x1 -> x0, blocking collectives: 9.71 us -> none  [per_device(): rank_rows = lax.all_gather(rank_per_token, 'mlp', axis=0, tiled=True)]
  transfers between devices with their start and end apart: 6 -> 0, of which waited for: 4 -> 0; matrix products, arithmetic and copies ran while one was open for 13% -> 0% of each run, Pallas kernels for 0% -> 0%
where the time goes in v2:
time: 237 us; the launch traced here: 236 us
  Pallas kernels  231 us (97%)
  local copies, waits for them, and re-layouts  5.53 us (2%)
    pallas_call x1, Pallas kernels, per_device(): pl.pallas_call(functools.partial(block_kernel, n_req, n_mlp), out_shape=(...  231 us

profile of v2, /device:TPU:19, one launch (start us, length us, event | category | flops | bytes accessed | tf_op | source)
XLA Modules:
  0.0 236.4 jit_solution(2514426934708150503)
XLA Ops:
  0.0 1.4 copy.12.names
  1.4 2.2 copy.11
  3.6 230.9 %shard_map.100 = (bf16[64,5120]{1,0:T(8,128)(2,1)}, bf16[8,256,1280]{2,1,0:T(8,128)(2,1)}) custom-call(bf16[64,5120]{1,0:T(8,128)(2,1)} %tokens.1, f32[1,5120]{1,0:T(1,128)} %bitcast.9, s32[64,1]{1,0:T(8,128)} %copy.12.names, bf16[5120,1792]{1,0:T(8,128)(2,1)} %gate_hbm.1, bf16[5120,1792]{1,0:T(8,128)(2,1)} %up_hbm.1, bf16[1792,1280]{1,0:T(8,128)(2,1)} %down_hbm.1, ...), custom_call_target="tpu_custom_call" | custom-call | tf_op jit(solution)/shard_map/pallas_call | solution.py:399
  234.4 2.0 copy.14

commit v3 on v2

--- a/solution.py
+++ b/solution.py
@@ -188,10 +188,13 @@
                 (r - sign, m),
             ).wait_recv()
 
+    middle = n_mlp // 2
+    order = [*range(middle), *range(middle + 1, n_mlp), middle]
+
     def tick(k):
         for step in range(n_req - 1, 0, -1):
-            slot = k - step
-            if 0 <= slot < n_mlp:
+            if 0 <= k - step < n_mlp:
+                slot = order[k - step]
                 for way in (0, 1):
                     hop_arrival(way, step, slot)
                     if step < n_req - 1:
@@ -202,7 +205,7 @@
             rk_out.at[slot], rk_in.at[slot], k_send.at[slot], k_recv.at[slot], (r, peer(slot))
         )
 
-    def compute(first, count, wait):
+    def compute(first, count, wait, ticks):
         size = count * rows
         at = pl.ds(first * rows, size)
         normed = x_all[at, 0:dim]
@@ -232,8 +235,14 @@
             hid[r, at, cols] = value.astype(BF16)
             return carry
 
-        lax.fori_loop(0, tiles, step, 0)
-        for slot in range(first, first + count):
+        reached = 0
+        for i, k in enumerate(ticks):
+            limit = tiles * (i + 1) // (len(ticks) + 1)
+            lax.fori_loop(reached, limit, step, 0)
+            reached = limit
+            tick(k)
+        lax.fori_loop(reached, tiles, step, 0)
+        for slot in order[first : first + count]:
             hop_start(0, 1, slot)
             hop_start(1, 1, slot)
         terms = lax.dot_general(
@@ -250,16 +259,16 @@
                 rk_out[slot] = term
                 rank_copy(slot).start()
 
-    compute(0, 1, True)
+    gather_copy(0).wait_recv()
+    gather_copy(1).start()
+    compute(0, 2, True, ())
     done = 0
-    for stage in range(bits):
+    for stage in range(1, bits):
         gather_copy(stage).wait_recv()
         if stage + 1 < bits:
             gather_copy(stage + 1).start()
-        compute(1 << stage, 1 << stage, False)
-        if stage + 1 < bits:
-            done = done + 1
-            tick(done)
+        compute(1 << stage, 1 << stage, False, (done + 1, done + 2))
+        done = done + 2
 
     down_copy.wait()
     narrow = tile_of(columns)
@@ -306,11 +315,11 @@
         if k > done:
             tick(k)
         while finished <= k - (n_req - 1) and finished < n_mlp:
-            down(finished)
+            down(order[finished])
             if finished >= 3:
-                collect(finished - 2)
+                collect(order[finished - 2])
             finished += 1
-    for slot in range(max(1, n_mlp - 2), n_mlp):
+    for slot in order[n_mlp - 2 :]:
         collect(slot)
 
     piece[...] = acc[...].astype(BF16)

time: 237 us -> 228 us (0.962)
  Pallas kernels: 231 us -> 221 us
    pallas_call x1, Pallas kernels: 231 us -> 221 us  [per_device(): pl.pallas_call(functools.partial(block_kernel, n_req, n_mlp), out_shape=(...]
where the time goes in v3:
time: 228 us; the launch traced here: 226 us
  Pallas kernels  221 us (97%)
  local copies, waits for them, and re-layouts  5.53 us (2%)
    pallas_call x1, Pallas kernels, per_device(): pl.pallas_call(functools.partial(block_kernel, n_req, n_mlp), out_shape=(...  221 us

profile of v3, /device:TPU:19, one launch (start us, length us, event | category | flops | bytes accessed | tf_op | source)
XLA Modules:
  0.0 226.2 jit_solution(16400903155659234652)
XLA Ops:
  0.0 1.4 copy.12.names
  1.4 2.2 copy.11
  3.6 220.7 %shard_map.100 = (bf16[64,5120]{1,0:T(8,128)(2,1)}, bf16[8,256,1280]{2,1,0:T(8,128)(2,1)}) custom-call(bf16[64,5120]{1,0:T(8,128)(2,1)} %tokens.1, f32[1,5120]{1,0:T(1,128)} %bitcast.9, s32[64,1]{1,0:T(8,128)} %copy.12.names, bf16[5120,1792]{1,0:T(8,128)(2,1)} %gate_hbm.1, bf16[5120,1792]{1,0:T(8,128)(2,1)} %up_hbm.1, bf16[1792,1280]{1,0:T(8,128)(2,1)} %down_hbm.1, ...), custom_call_target="tpu_custom_call" | custom-call | tf_op jit(solution)/shard_map/pallas_call | solution.py:408
  224.2 2.0 copy.14
